TPU v7x, 256 devices: a whole 4x4x8 slice. The times are simulated.
256 devices in a mesh: tp: 32 (over z, x_lo, core), dp: 8 (over x_hi, y).
Axes of the slice: x: 4 (x_hi: 2, x_lo: 2; x = x_hi * 2 + x_lo), y: 4, z: 8, core: 2. Of those that a mesh axis runs over, the one named last changes fastest.
Arguments:
- forget_inputs: bfloat16 [4096, 8192], P(('tp', 'dp')), may hold values from -6 to 6
- gate_pre: bfloat16 [4096, 16384], P('dp', 'tp'), may hold values from -6 to 6
- up_pre: bfloat16 [4096, 16384], P('dp', 'tp'), may hold values from -6 to 6
- hidden_grad: bfloat16 [4096, 16384], P('dp', 'tp'), may hold values from -6 to 6
- gate_weight: bfloat16 [8192, 16384], P('dp', 'tp'), may hold values from -0.0625 to 0.0625
- up_weight: bfloat16 [8192, 16384], P('dp', 'tp'), may hold values from -0.0625 to 0.0625
- retain_gate: float32 [8192, 16384], P('dp', 'tp'), may hold values from 0.002 to 0.2
- retain_up: float32 [8192, 16384], P('dp', 'tp'), may hold values from 0.002 to 0.2
Outputs:
- new_gate: bfloat16 [8192, 16384], P('dp', 'tp')
- new_up: bfloat16 [8192, 16384], P('dp', 'tp')
All inputs are finite; a program needn't handle non-finite values.
Results may differ from a plain program's by a relative error of at most 0.0064.
Values may be sent and summed in bfloat16 or wider, within the bound.
No kernel may reach another device: no remote copies, remote signals or barrier semaphores. Data moves between devices by JAX's collectives and lax.ppermute only.
A program may use at most 128 MiB of HBM per device.

v0:
```python
import jax
import jax.numpy as jnp
from jax import lax
from jax.sharding import PartitionSpec as P

select_ratio = 10.0
dampen_ratio = 10.0


def accumulate(piece, deltas):
    return lax.dot_general(
        piece, deltas, (((0,), (0,)), ((), ())), preferred_element_type=jnp.float32
    )


def dampened(weight, retain, summed, count):
    forget = summed * summed / count
    factor = dampen_ratio * retain / jnp.maximum(forget, select_ratio * retain)
    return (weight.astype(jnp.float32) * factor).astype(jnp.bfloat16)


def body(
    forget_inputs, gate_pre, up_pre, hidden_grad, gate_weight, up_weight, retain_gate, retain_up
):
    gate_val = gate_pre.astype(jnp.float32)
    up_val = up_pre.astype(jnp.float32)
    grad_val = hidden_grad.astype(jnp.float32)
    sig = jax.nn.sigmoid(gate_val)
    gate_delta = (grad_val * up_val * sig * (1.0 + gate_val * (1.0 - sig))).astype(jnp.bfloat16)
    up_delta = (grad_val * gate_val * sig).astype(jnp.bfloat16)
    gate_all, up_all = (
        lax.all_gather(gate_delta, "dp", axis=0, tiled=True),
        lax.all_gather(up_delta, "dp", axis=0, tiled=True),
    )
    columns = lax.all_to_all(forget_inputs, "dp", split_axis=1, concat_axis=0, tiled=True)
    count = float(gate_all.shape[0])
    gate_sum = accumulate(lax.all_gather(columns, "tp", axis=0, tiled=True), gate_all)
    up_sum = accumulate(lax.all_gather(columns, "tp", axis=0, tiled=True), up_all)
    new_gate = dampened(gate_weight, retain_gate, gate_sum, count)
    new_up = dampened(up_weight, retain_up, up_sum, count)
    return (new_gate, new_up)


def solution(mesh):
    placed = (
        P(("tp", "dp"), None),
        P("dp", "tp"),
        P("dp", "tp"),
        P("dp", "tp"),
        P("dp", "tp"),
        P("dp", "tp"),
        P("dp", "tp"),
        P("dp", "tp"),
    )
    return jax.shard_map(
        body, mesh=mesh, in_specs=placed, out_specs=(P("dp", "tp"), P("dp", "tp")), check_vma=False
    )
```

profile of v0, /device:TPU:1, one launch (start us, length us, event | category | flops | bytes accessed | tf_op | source)
XLA Modules:
  0.0 259.4 jit_solution(13563033080113747796)
XLA Ops:
  7.2 0.0 copy-start.7
  7.2 0.0 copy-start
  7.2 0.0 all-gather.4.cloned.1.call-start
  7.2 3.0 %fusion.12 = (bf16[512,512]{1,0:T(8,128)(2,1)}, bf16[512,512]{1,0:T(8,128)(2,1)}) fusion(bf16[512,512]{1,0:T(8,128)(2,1)} %param.9, bf16[512,512]{1,0:T(8,128)(2,1)} %param.11, bf16[512,512]{1,0:T(8,128)(2,1)} %param.10), kind=kLoop, calls=%fused_computation.18 | loop fusion | flops 4194304 | bytes 2621440 | tf_op jit(solution)/shard_map/convert_element_type | solution.py:30
  10.2 0.0 all-gather.4.cloned.1.call-update
  10.3 0.0 all-gather.6.cloned.1.call-start
  10.4 15.0 %all_to_all.19 = bf16[16,8,1024]{2,0,1:T(8,128)(2,1)} all-to-all(bf16[16,8,1024]{2,0,1:T(8,128)(2,1)S(1)} %bitcast.16), channel_id=1, replica_groups=mesh['tp'=32,'dp'=8] {'dp'}, dimensions={1} | all-to-all | bytes 524288 | tf_op jit(solution)/shard_map/all_to_all | solution.py:35
  25.3 0.0 all-gather.6.cloned.1.call-update
  25.3 0.0 all-gather.8.cloned.1.call-start
  25.4 0.7 all-gather.8.cloned.1.call-update
  26.1 0.0 copy-start.4
  26.1 1.9 copy.30
  28.0 0.0 copy-done.4
  28.0 1.3 copy.29
  29.3 0.7 copy-done.1
  30.0 1.8 copy.33
  31.9 1.3 copy.32
  33.2 57.3 %all-gather.4.cloned.1.call-done = bf16[4096,512]{1,0:T(8,128)(2,1)} async-done(((bf16[512,512]{1,0:T(8,128)(2,1)}), bf16[4096,512]{1,0:T(8,128)(2,1)}) %all-gather.4.cloned.1.call-update) | async-done | bytes 4194320 | tf_op jit(solution)/shard_map/all_gather | solution.py:32
  90.4 72.6 %all-gather.6.cloned.1.call-done = bf16[4096,1024]{1,0:T(8,128)(2,1)} async-done(((bf16[128,1024]{1,0:T(8,128)(2,1)}), bf16[4096,1024]{1,0:T(8,128)(2,1)}) %all-gather.6.cloned.1.call-update) | async-done | bytes 8388624 | tf_op jit(solution)/shard_map/all_gather | solution.py:37
  163.1 10.7 %fusion.1 = bf16[1024,512]{0,1:T(8,128)(2,1)} fusion(f32[1024,512]{0,1:T(8,128)S(1)} %copy-done.3, bf16[1024,512]{0,1:T(8,128)(2,1)} %copy.29, bf16[4096,512]{1,0:T(8,128)(2,1)} %all-gather.4.cloned.1.call-done, bf16[4096,1024]{1,0:T(8,128)(2,1)} %all-gather.6.cloned.1.call-done), kind=kOutput, calls=%fused_computation.3 | convolution fusion | flops 4299161600 | bytes 16777216 | tf_op jit(solution)/shard_map/dot_general | solution.py:11
  173.8 2.4 copy.34
  176.2 63.8 %all-gather.8.cloned.1.call-done = bf16[4096,512]{1,0:T(8,128)(2,1)} async-done(((bf16[512,512]{1,0:T(8,128)(2,1)}), bf16[4096,512]{1,0:T(8,128)(2,1)}) %all-gather.8.cloned.1.call-update) | async-done | bytes 4194320 | tf_op jit(solution)/shard_map/all_gather | solution.py:33
  240.0 10.6 %fusion.3 = bf16[1024,512]{0,1:T(8,128)(2,1)} fusion(f32[1024,512]{0,1:T(8,128)S(1)} %copy-done.2, bf16[1024,512]{0,1:T(8,128)(2,1)S(1)} %copy-done.6, bf16[4096,512]{1,0:T(8,128)(2,1)} %all-gather.8.cloned.1.call-done, bf16[4096,1024]{1,0:T(8,128)(2,1)} %all-gather.6.cloned.1.call-done), kind=kOutput, calls=%fused_computation.5 | convolution fusion | flops 4299161600 | bytes 16777216 | tf_op jit(solution)/shard_map/dot_general | solution.py:11
  250.6 2.3 copy.35
  (12 shorter events, 0.0 us)
Async XLA Ops:
  7.2 3.2 %copy-start.7 = (bf16[16,8192]{1,0:T(8,128)(2,1)S(1)}, bf16[16,8192]{1,0:T(8,128)(2,1)}, u32[]{:S(2)}) copy-start(bf16[16,8192]{1,0:T(8,128)(2,1)} %param.8) | copy-start | bytes 786436
  7.2 18.9 %copy-start = (f32[1024,512]{1,0:T(8,128)S(1)}, f32[1024,512]{1,0:T(8,128)}, u32[]{:S(2)}) copy-start(f32[1024,512]{1,0:T(8,128)} %param.14) | copy-start | bytes 6291460
  7.2 83.2 %all-gather.4.cloned.1.call-start = ((), (), s32[]{:S(2)}) async-start(), calls=%async_computation.1 | async-start | bytes 4718592 | tf_op jit(solution)/shard_map/all_gather | solution.py:32
  10.3 152.8 %all-gather.6.cloned.1.call-start = ((), (), s32[]{:S(2)}) async-start(), calls=%async_computation.2 | async-start | bytes 8650752 | tf_op jit(solution)/shard_map/all_gather | solution.py:37
  25.3 214.7 %all-gather.8.cloned.1.call-start = ((), (), s32[]{:S(2)}) async-start(), calls=%async_computation.3 | async-start | bytes 4718592 | tf_op jit(solution)/shard_map/all_gather | solution.py:33
  26.1 1.9 copy-start.4
  28.0 2.0 copy-start.1
  30.0 1.8 copy-start.5
  31.8 131.2 %copy-start.3 = (f32[1024,512]{0,1:T(8,128)S(1)}, f32[1024,512]{0,1:T(8,128)}, u32[]{:S(2)}) copy-start(f32[1024,512]{0,1:T(8,128)} %copy.30) | copy-start | bytes 6291460
  163.1 76.9 %copy-start.6 = (bf16[1024,512]{0,1:T(8,128)(2,1)S(1)}, bf16[1024,512]{0,1:T(8,128)(2,1)}, u32[]{:S(2)}) copy-start(bf16[1024,512]{0,1:T(8,128)(2,1)} %copy.32) | copy-start | bytes 3145732
  173.8 66.2 %copy-start.2 = (f32[1024,512]{0,1:T(8,128)S(1)}, f32[1024,512]{0,1:T(8,128)}, u32[]{:S(2)}) copy-start(f32[1024,512]{0,1:T(8,128)} %copy.33) | copy-start | bytes 6291460
Sparse Core Ops, SparseCore 0:
  11.2 79.1 all-gather.3
  92.3 70.7 all-gather.5
  165.7 74.2 all-gather.7
where the time goes:
time: 260 us; the launch traced here: 259 us
  waiting for transfers between devices  194 us (75%)
  matrix products  21.3 us (8%)
  blocking collectives  15 us (6%)
  between operations  13.8 us (5%)
  local copies, waits for them, and re-layouts  11.8 us (5%)
  other arithmetic  3.02 us (1%)
    all_gather x1, waiting for transfers between devices, body(): lax.all_gather(columns, 'tp', axis=0, tiled=True)  72.6 us
    all_gather x1, waiting for transfers between devices, body(): lax.all_gather(up_delta, 'dp', axis=0, tiled=True)  63.8 us
    all_gather x1, waiting for transfers between devices, body(): lax.all_gather(gate_delta, 'dp', axis=0, tiled=True)  57.3 us
    dot_general x2, matrix products, accumulate(): lax.dot_general(piece, deltas, (((0,), (0,)), ((), ())), preferred_elemen...  21.3 us
    all_to_all x1, blocking collectives, body(): lax.all_to_all(forget_inputs, 'dp', split_axis=1, concat_axis=0, tiled=True)  15 us
    unnamed x22, local copies, waits for them, and re-layouts  11.8 us
  transfers between devices with their start and end apart: 3, of which 3 were waited for; matrix products, arithmetic and copies ran while one was open for 8% of the time, Pallas kernels for 0%

commit v1 on v0

--- a/solution.py
+++ b/solution.py
@@ -22,6 +22,13 @@
 def body(
     forget_inputs, gate_pre, up_pre, hidden_grad, gate_weight, up_weight, retain_gate, retain_up
 ):
+
+    def order_patches_on(a0):
+        r_now = lax.axis_size("dp")
+        z1 = jnp.stack([a0] * r_now)
+        u_next = lax.all_to_all(z1, axis_name="dp", split_axis=0, concat_axis=0)
+        return jnp.concatenate(u_next, 0)
+
     gate_val = gate_pre.astype(jnp.float32)
     up_val = up_pre.astype(jnp.float32)
     grad_val = hidden_grad.astype(jnp.float32)
@@ -29,7 +36,7 @@
     gate_delta = (grad_val * up_val * sig * (1.0 + gate_val * (1.0 - sig))).astype(jnp.bfloat16)
     up_delta = (grad_val * gate_val * sig).astype(jnp.bfloat16)
     gate_all, up_all = (
-        lax.all_gather(gate_delta, "dp", axis=0, tiled=True),
+        order_patches_on(gate_delta),
         lax.all_gather(up_delta, "dp", axis=0, tiled=True),
     )
     columns = lax.all_to_all(forget_inputs, "dp", split_axis=1, concat_axis=0, tiled=True)

time: 260 us -> 218 us (0.84)
  waiting for transfers between devices: 194 us -> 145 us
  starting transfers between devices: 0.12 us -> 4.79 us
  local copies, waits for them, and re-layouts: 11.8 us -> 15.1 us
    all_to_all x0 -> x1, waiting for transfers between devices: none -> 81.7 us  [order_patches_on(): u_next = lax.all_to_all(z1, axis_name='dp', split_axis=0, concat_axis=0)]
    all_gather x1, waiting for transfers between devices: 72.6 us -> 0.49 us  [body(): lax.all_gather(columns, 'tp', axis=0, tiled=True)]
    all_gather x1 -> x0, waiting for transfers between devices: 57.3 us -> none  [body(): lax.all_gather(gate_delta, 'dp', axis=0, tiled=True)]
    all_to_all x0 -> x1, starting transfers between devices: none -> 4.72 us  [order_patches_on(): u_next = lax.all_to_all(z1, axis_name='dp', split_axis=0, concat_axis=0)]
    unnamed x22 -> x20, local copies, waits for them, and re-layouts: 11.8 us -> 11.9 us
  transfers between devices with their start and end apart: 3 -> 3, of which waited for: 3 -> 3; matrix products, arithmetic and copies ran while one was open for 8% -> 11% of each run, Pallas kernels for 0% -> 0%
where the time goes in v1:
time: 218 us
  waiting for transfers between devices  145 us (67%)
  matrix products  21.3 us (10%)
  local copies, waits for them, and re-layouts  15.1 us (7%)
  blocking collectives  15 us (7%)
  between operations  14.1 us (6%)
  starting transfers between devices  4.79 us (2%)
  other arithmetic  2.7 us (1%)
    all_to_all x1, waiting for transfers between devices, order_patches_on(): u_next = lax.all_to_all(z1, axis_name='dp', split_axis=0, concat_axis=0)  81.7 us
    all_gather x1, waiting for transfers between devices, body(): lax.all_gather(up_delta, 'dp', axis=0, tiled=True)  62.9 us
    dot_general x2, matrix products, accumulate(): lax.dot_general(piece, deltas, (((0,), (0,)), ((), ())), preferred_elemen...  21.3 us
    all_to_all x1, blocking collectives, body(): lax.all_to_all(forget_inputs, 'dp', split_axis=1, concat_axis=0, tiled=True)  15 us
    unnamed x20, local copies, waits for them, and re-layouts  11.9 us
    all_to_all x1, starting transfers between devices, order_patches_on(): u_next = lax.all_to_all(z1, axis_name='dp', split_axis=0, concat_axis=0)  4.72 us
  transfers between devices with their start and end apart: 3, of which 3 were waited for; matrix products, arithmetic and copies ran while one was open for 11% of the time, Pallas kernels for 0%

profile of v1, /device:TPU:1, one launch (start us, length us, event | category | flops | bytes accessed | tf_op | source)
XLA Modules:
  0.0 218.2 jit_solution(3457463135117285330)
XLA Ops:
  7.2 0.0 all-gather.3.cloned.1.call-start
  7.2 1.0 copy.38
  8.2 15.0 %all_to_all.24 = bf16[16,8,1024]{2,0,1:T(8,128)(2,1)} all-to-all(bf16[16,8,1024]{2,0,1:T(8,128)(2,1)S(1)} %bitcast.17), channel_id=1, replica_groups=mesh['tp'=32,'dp'=8] {'dp'}, dimensions={1} | all-to-all | bytes 524288 | tf_op jit(solution)/shard_map/all_to_all | solution.py:42
  23.1 0.0 all-gather.3.cloned.1.call-update
  23.2 0.0 all-gather.5.cloned.1.call-start
  23.2 2.7 %fusion.12 = (bf16[512,512]{1,0:T(8,128)(2,1)}, bf16[512,512]{1,0:T(8,128)(2,1)S(1)}) fusion(bf16[512,512]{1,0:T(8,128)(2,1)} %param.9, bf16[512,512]{1,0:T(8,128)(2,1)} %param.11, bf16[512,512]{1,0:T(8,128)(2,1)} %param.10), kind=kLoop, calls=%fused_computation.18 | loop fusion | flops 4194304 | bytes 2621440 | tf_op jit(solution)/shard_map/convert_element_type | solution.py:37
  25.9 0.0 all-gather.5.cloned.1.call-update
  25.9 2.3 %stack.2 = bf16[8,512,512]{2,1,0:T(8,128)(2,1)} broadcast(bf16[512,512]{1,0:T(8,128)(2,1)S(1)} %get-tuple-element.11), dimensions={1,2} | broadcast | bytes 4718592 | tf_op jit(solution)/shard_map/stack | solution.py:28
  28.2 4.7 %all-to-all-start = ((bf16[8,512,512]{2,1,0:T(8,128)(2,1)}), bf16[8,512,512]{2,1,0:T(8,128)(2,1)}, u32[]{:S(2)}, u32[]{:S(2)}) async-start(bf16[8,512,512]{2,1,0:T(8,128)(2,1)} %stack.2), calls=%async_computation | async-start | bytes 8388608 | tf_op jit(solution)/shard_map/all_to_all | solution.py:29
  33.0 0.0 copy-done
  33.0 0.0 copy-start.4
  33.0 1.9 copy.30
  34.9 1.3 copy.29
  36.2 0.8 copy-done.1
  37.0 1.8 copy.33
  38.8 0.0 copy-done.5
  38.8 1.4 copy.32
  40.2 81.7 %all-to-all-done = bf16[8,512,512]{2,1,0:T(8,128)(2,1)} async-done(((bf16[8,512,512]{2,1,0:T(8,128)(2,1)}), bf16[8,512,512]{2,1,0:T(8,128)(2,1)}, u32[]{:S(2)}, u32[]{:S(2)}) %all-to-all-start) | async-done | bytes 4194336 | tf_op jit(solution)/shard_map/all_to_all | solution.py:29
  121.9 0.5 all-gather.3.cloned.1.call-done
  122.4 10.7 %fusion.1 = bf16[1024,512]{0,1:T(8,128)(2,1)} fusion(f32[1024,512]{0,1:T(8,128)S(1)} %copy-done.3, bf16[1024,512]{0,1:T(8,128)(2,1)} %copy.29, bf16[4096,512]{1,0:T(8,128)(2,1)} %bitcast, bf16[4096,1024]{1,0:T(8,128)(2,1)} %all-gather.3.cloned.1.call-done), kind=kOutput, calls=%fused_computation.3 | convolution fusion | flops 4299161600 | bytes 16777216 | tf_op jit(solution)/shard_map/dot_general | solution.py:11
  133.1 2.4 %copy.34 = bf16[1024,512]{1,0:T(8,128)(2,1)} copy(bf16[1024,512]{0,1:T(8,128)(2,1)} %fusion.1) | data formatting | bytes 2097152
  135.5 62.9 %all-gather.5.cloned.1.call-done = bf16[4096,512]{1,0:T(8,128)(2,1)} async-done(((bf16[512,512]{1,0:T(8,128)(2,1)}), bf16[4096,512]{1,0:T(8,128)(2,1)}) %all-gather.5.cloned.1.call-update) | async-done | bytes 4194320 | tf_op jit(solution)/shard_map/all_gather | solution.py:40
  198.5 10.6 %fusion.3 = bf16[1024,512]{0,1:T(8,128)(2,1)} fusion(f32[1024,512]{0,1:T(8,128)S(1)} %copy-done.2, bf16[1024,512]{0,1:T(8,128)(2,1)S(1)} %copy-done.6, bf16[4096,512]{1,0:T(8,128)(2,1)} %all-gather.5.cloned.1.call-done, bf16[4096,1024]{1,0:T(8,128)(2,1)} %all-gather.3.cloned.1.call-done), kind=kOutput, calls=%fused_computation.5 | convolution fusion | flops 4299161600 | bytes 16777216 | tf_op jit(solution)/shard_map/dot_general | solution.py:11
  209.0 2.3 %copy.35 = bf16[1024,512]{1,0:T(8,128)(2,1)} copy(bf16[1024,512]{0,1:T(8,128)(2,1)} %fusion.3) | data formatting | bytes 2097152
  (10 shorter events, 0.0 us)
Async XLA Ops:
  7.2 115.2 %all-gather.3.cloned.1.call-start = ((), (), s32[]{:S(2)}) async-start(), calls=%async_computation.2 | async-start | bytes 8650752 | tf_op jit(solution)/shard_map/all_gather | solution.py:44
  23.2 175.3 %all-gather.5.cloned.1.call-start = ((), (), s32[]{:S(2)}) async-start(), calls=%async_computation.3 | async-start | bytes 4718592 | tf_op jit(solution)/shard_map/all_gather | solution.py:40
  28.2 4.7 %copy-start = (f32[1024,512]{1,0:T(8,128)S(1)}, f32[1024,512]{1,0:T(8,128)}, u32[]{:S(2)}) copy-start(f32[1024,512]{1,0:T(8,128)} %param.14) | copy-start | bytes 6291460
  28.2 93.6 %all-to-all-start = ((bf16[8,512,512]{2,1,0:T(8,128)(2,1)}), bf16[8,512,512]{2,1,0:T(8,128)(2,1)}, u32[]{:S(2)}, u32[]{:S(2)}) async-start(bf16[8,512,512]{2,1,0:T(8,128)(2,1)} %stack.2), calls=%async_computation | async-start | bytes 8388608 | tf_op jit(solution)/shard_map/all_to_all | solution.py:29
  33.0 1.9 copy-start.4
  34.9 2.1 copy-start.1
  36.9 1.8 copy-start.5
  38.8 83.6 %copy-start.3 = (f32[1024,512]{0,1:T(8,128)S(1)}, f32[1024,512]{0,1:T(8,128)}, u32[]{:S(2)}) copy-start(f32[1024,512]{0,1:T(8,128)} %copy.30) | copy-start | bytes 6291460
  122.4 76.1 %copy-start.6 = (bf16[1024,512]{0,1:T(8,128)(2,1)S(1)}, bf16[1024,512]{0,1:T(8,128)(2,1)}, u32[]{:S(2)}) copy-start(bf16[1024,512]{0,1:T(8,128)(2,1)} %copy.32) | copy-start | bytes 3145732
  133.1 65.4 %copy-start.2 = (f32[1024,512]{0,1:T(8,128)S(1)}, f32[1024,512]{0,1:T(8,128)}, u32[]{:S(2)}) copy-start(f32[1024,512]{0,1:T(8,128)} %copy.33) | copy-start | bytes 6291460
Sparse Core Ops, SparseCore 0:
  23.3 99.0 all-gather.2
  125.0 73.3 all-gather.4
